TPU v7x, 32 devices: a whole 2x2x4 slice. The times are simulated.
32 devices in a mesh: expert: 8 (over y, x, core), dp: 4 (over z).
Axes of the slice: x: 2, y: 2, z: 4, core: 2. Of those that a mesh axis runs over, the one named last changes fastest.
Arguments:
- out_grad: bfloat16 [512, 2048], P(('expert', 'dp')), may hold values from -2.5 to 2.5
- expert_ids: int32 [512, 8], P(('expert', 'dp')), may hold values from 0 to 15, all different within a row; in each aligned block of 16 rows (0 to 15, 16 to 31, ...) at most 16 rows name the same one
- route_weights: float32 [512, 8], P(('expert', 'dp')), may hold values from 0.1 to 1
- saved_hidden: bfloat16 [16, 512, 768], P('expert', 'dp'), may hold values from -3 to 3
- w_down: bfloat16 [16, 768, 2048], P('expert'), may hold values from -0.21875 to 0.21875
- swap_flags: int32 [8, 4], P(None, 'dp'), may hold values from 0 to 1, as said below
Outputs:
- hidden_grad: bfloat16 [16, 512, 768], P('expert', 'dp')
- down_grad: bfloat16 [16, 768, 2048], P('expert', None, 'dp')
Inputs may be any that keep to these rules, and one draw needn't show every extreme that they name: `expert_ids`: among the tokens of one device (aligned blocks of 16 tokens) no expert is chosen more than 16 times, and in every draw some expert is chosen exactly 16 times by one device. swap_flags[i, g] equals swap_flags[i + h, g] with h half of 8; rows 0 and h - 1 carry 1 in every group, the other rows are independent bits.
All inputs are finite; a program needn't handle non-finite values.
Results may differ from a plain program's by a relative error of at most 0.014.
Values may be sent and summed in bfloat16 or wider, within the bound.
A program may use at most 64 MiB of HBM per device.

v0:
```python
import jax
import jax.numpy as jnp
from jax import lax
from jax.sharding import PartitionSpec as P


def from_partner(shard, axis, stride):
    return lax.ppermute(shard, axis, [(i, i ^ 1 << stride) for i in range(lax.axis_size(axis))])


def body(out_grad, expert_ids, route_weights, saved_hidden, w_down, swap_flags):
    host_count = lax.axis_size("expert")
    my_host = lax.axis_index("expert")
    local_experts, slot_rows, hidden_units = saved_hidden.shape
    capacity = slot_rows // host_count
    expert_count = local_experts * host_count
    model_width = out_grad.shape[1]
    chosen = expert_ids.reshape(-1)
    expert_range = jnp.arange(expert_count, dtype=jnp.int32)
    one_hot = (chosen[:, None] == expert_range[None, :]).astype(jnp.int32)
    position = jnp.sum((jnp.cumsum(one_hot, axis=0) - 1) * one_hot, axis=1)
    dest_flat = chosen * capacity + position
    scaled = (route_weights[:, :, None] * out_grad[:, None, :].astype(jnp.float32)).astype(
        jnp.bfloat16
    )
    scaled = scaled.reshape(-1, model_width)
    send_rows = (
        jnp.zeros((expert_count * capacity, model_width), jnp.bfloat16).at[dest_flat].set(scaled)
    )
    send_rows = send_rows.reshape(expert_count, capacity, model_width)
    received = lax.all_to_all(send_rows, "expert", split_axis=0, concat_axis=1, tiled=True)
    hidden_grad = jnp.einsum(
        "srd,sfd->srf", received, w_down, preferred_element_type=jnp.float32
    ).astype(jnp.bfloat16)
    width_rows = lax.all_to_all(received, "dp", split_axis=2, concat_axis=1, tiled=True)
    share_width = width_rows.shape[2]
    segment = lax.all_gather(saved_hidden, "dp", axis=1, tiled=True)
    row_count = segment.shape[1]
    blocks = row_count // slot_rows
    product = jnp.einsum(
        "sgrf,sgrd->sgfd",
        segment.reshape(local_experts, blocks, slot_rows, hidden_units),
        width_rows.reshape(local_experts, blocks, slot_rows, share_width),
        preferred_element_type=jnp.float32,
    )
    narrow = lax.optimization_barrier(product.astype(jnp.bfloat16))
    summed = jnp.sum(narrow.astype(jnp.float32), axis=1)
    grad_local = summed.astype(jnp.bfloat16)
    pair_bit = (host_count // 2).bit_length() - 1
    incoming = from_partner(grad_local[1], "expert", pair_bit)
    host_range = jnp.arange(host_count, dtype=jnp.int32)
    own_flag = jnp.sum(jnp.where(host_range == my_host, swap_flags[:, 0], 0))
    second = jnp.where(own_flag == 1, incoming, grad_local[1])
    down_grad = jnp.stack([grad_local[0], second])
    return (hidden_grad, down_grad)


def solution(mesh):
    in_specs = (
        P(("expert", "dp"), None),
        P(("expert", "dp"), None),
        P(("expert", "dp"), None),
        P("expert", "dp", None),
        P("expert", None, None),
        P(None, "dp"),
    )
    out_specs = (P("expert", "dp", None), P("expert", None, "dp"))
    return jax.shard_map(body, mesh=mesh, in_specs=in_specs, out_specs=out_specs, check_vma=False)
```

profile of v0, /device:TPU:0, one launch (start us, length us, event | category | flops | bytes accessed | tf_op | source)
XLA Modules:
  0.0 122.3 jit_solution(15031497859029938145)
XLA Ops:
  7.2 0.7 broadcast_multiply_fusion
  7.9 0.8 copy.18
  8.6 0.1 copy.17
  8.7 0.1 mul.39
  8.8 0.1 eq.24
  8.9 0.1 fusion.6
  9.0 0.2 reduce_window_sum.11
  9.1 0.2 select_reduce_fusion
  9.3 0.9 convert_element_type.23
  10.2 0.8 copy.19
  10.9 0.1 mul.41
  11.0 2.5 %scatter_custom_fusion = bf16[256,2048]{1,0:T(8,128)(2,1)} fusion(s32[128]{0:T(128)S(1)} %fusion.8, f32[16,2048]{1,0:T(8,128)S(1)} %convert_element_type.23, f32[128]{0:T(128)S(1)} %mul.41, bf16[]{:T(256)} %constant.8.clone.1), kind=kCustom, calls=%fused_computation.8 | custom fusion | flops 524288 | bytes 1180162 | tf_op jit(solution)/shard_map/scatter | solution.py:28
  13.5 5.2 %all-to-all-start = ((bf16[16,16,2048]{2,1,0:T(8,128)(2,1)}), bf16[16,16,2048]{2,1,0:T(8,128)(2,1)S(1)}, u32[]{:S(2)}, u32[]{:S(2)}) async-start(bf16[16,16,2048]{2,1,0:T(8,128)(2,1)} %bitcast.3), calls=%async_computation | async-start | bytes 2097152 | tf_op jit(solution)/shard_map/all_to_all | solution.py:31
  18.7 0.0 all-gather.2.cloned.1.call-start
  18.8 0.7 all-gather.2.cloned.1.call-update
  19.5 14.6 %all-to-all-done = bf16[16,16,2048]{2,1,0:T(8,128)(2,1)S(1)} async-done(((bf16[16,16,2048]{2,1,0:T(8,128)(2,1)}), bf16[16,16,2048]{2,1,0:T(8,128)(2,1)S(1)}, u32[]{:S(2)}, u32[]{:S(2)}) %all-to-all-start) | async-done | bytes 1048608 | tf_op jit(solution)/shard_map/all_to_all | solution.py:31
  34.1 0.1 copy.20
  34.2 0.8 copy.21
  35.0 47.0 %all_to_all.33 = bf16[2,128,2048]{1,0,2:T(2,128)(2,1)S(1)} all-to-all(bf16[2,128,2048]{1,0,2:T(2,128)(2,1)S(1)} %copy.21), channel_id=1, replica_groups=mesh['expert'=8,'dp'=4] {'dp'}, dimensions={2} | all-to-all | bytes 2097152 | tf_op jit(solution)/shard_map/all_to_all | solution.py:35
  82.0 0.1 copy.22
  82.2 0.0 all-gather.2.cloned.1.call-done
  82.2 5.9 %convert_bitcast_fusion = bf16[2,4,768,512]{2,3,1,0:T(8,128)(2,1)} fusion(bf16[2,4,128,512]{2,3,1,0:T(8,128)(2,1)S(1)} %bitcast.36, bf16[2,4,128,768]{3,2,1,0:T(8,128)(2,1)} %bitcast.38), kind=kOutput, calls=%fused_computation.1 | convolution fusion | flops 808452096 | bytes 8912896 | tf_op jit(solution)/shard_map/sgrf,sgrd->sgfd/dot_general | solution.py:40
  88.0 4.3 %reduce_sum.34 = bf16[2,768,512]{1,2,0:T(8,128)(2,1)S(1)} reduce(bf16[2,4,768,512]{2,3,1,0:T(8,128)(2,1)} %convert_bitcast_fusion, bf16[]{:T(256)} %constant.8.clone.1), dimensions={1}, to_apply=%region_3.4 | reduce | flops 2359296 | bytes 7864322 | tf_op jit(solution)/shard_map/reduce_sum | solution.py:47
  92.4 0.0 copy-start
  92.4 1.0 fusion.9
  93.4 1.5 %collective-permute-start = (bf16[768,512]{0,1:T(8,128)(2,1)}, bf16[768,512]{0,1:T(8,128)(2,1)}, u32[]{:S(2)}, u32[]{:S(2)}) collective-permute-start(bf16[768,512]{0,1:T(8,128)(2,1)} %get-tuple-element.5), channel_id=1, source_target_pairs={{0,16},{4,20},{8,24},{12,28},{16,0},{20,4},{24,8},{28,12},{1,17},{... | collective-permute-start | bytes 2359304 | tf_op jit(solution)/shard_map/ppermute | solution.py:8
  94.8 0.6 fusion.7
  96.1 5.7 %convolution_convert_fusion = bf16[2,128,768]{2,1,0:T(8,128)(2,1)} fusion(bf16[2,128,2048]{2,1,0:T(8,128)(2,1)S(1)} %bitcast.35, bf16[2,768,2048]{2,1,0:T(8,128)(2,1)} %param.10), kind=kOutput, calls=%fused_computation.3 | convolution fusion | flops 805502976 | bytes 7733248 | tf_op jit(solution)/shard_map/srd,sfd->srf/dot_general | solution.py:32
  101.8 10.6 %collective-permute-done = bf16[768,512]{0,1:T(8,128)(2,1)} collective-permute-done((bf16[768,512]{0,1:T(8,128)(2,1)}, bf16[768,512]{0,1:T(8,128)(2,1)}, u32[]{:S(2)}, u32[]{:S(2)}) %collective-permute-start) | collective-permute-done | bytes 786464 | tf_op jit(solution)/shard_map/ppermute | solution.py:8
  112.5 1.2 select_bitcast_fusion
  113.7 0.1 pad_maximum_fusion
  113.9 1.6 %copy.23 = bf16[2,768,512]{2,1,0:T(8,128)(2,1)} copy(bf16[2,768,512]{1,2,0:T(8,128)(2,1)S(1)} %pad_maximum_fusion) | data formatting | bytes 3145728
  (2 shorter events, 0.0 us)
Async XLA Ops:
  13.5 20.6 %all-to-all-start = ((bf16[16,16,2048]{2,1,0:T(8,128)(2,1)}), bf16[16,16,2048]{2,1,0:T(8,128)(2,1)S(1)}, u32[]{:S(2)}, u32[]{:S(2)}) async-start(bf16[16,16,2048]{2,1,0:T(8,128)(2,1)} %bitcast.3), calls=%async_computation | async-start | bytes 2097152 | tf_op jit(solution)/shard_map/all_to_all | solution.py:31
  18.7 63.4 %all-gather.2.cloned.1.call-start = ((), (), s32[]{:S(2)}) async-start(), calls=%async_computation.2 | async-start | bytes 1966080 | tf_op jit(solution)/shard_map/all_gather | solution.py:37
  92.4 2.5 %copy-start = (s32[8,1]{0,1:T(1,128)S(1)}, s32[8,1]{0,1:T(1,128)}, u32[]{:S(2)}) copy-start(s32[8,1]{0,1:T(1,128)} %param.11) | copy-start | bytes 100
  93.4 19.1 %collective-permute-start = (bf16[768,512]{0,1:T(8,128)(2,1)}, bf16[768,512]{0,1:T(8,128)(2,1)}, u32[]{:S(2)}, u32[]{:S(2)}) collective-permute-start(bf16[768,512]{0,1:T(8,128)(2,1)} %get-tuple-element.5), channel_id=1, source_target_pairs={{0,16},{4,20},{8,24},{12,28},{16,0},{20,4},{24,8},{28,12},{1,17},{... | collective-permute-start | bytes 2359304 | tf_op jit(solution)/shard_map/ppermute | solution.py:8
Sparse Core Ops, SparseCore 0:
  21.1 59.1 all-gather.1
where the time goes:
time: 123 us; the launch traced here: 122 us
  blocking collectives  47 us (38%)
  waiting for transfers between devices  26 us (21%)
  between operations  14.8 us (12%)
  matrix products  11.6 us (9%)
  other arithmetic  10.8 us (9%)
  starting transfers between devices  6.71 us (5%)
  local copies, waits for them, and re-layouts  5.44 us (4%)
    all_to_all x1, blocking collectives, body(): lax.all_to_all(received, 'dp', split_axis=2, concat_axis=1, tiled=True)  47 us
    all_to_all x1, waiting for transfers between devices, body(): lax.all_to_all(send_rows, 'expert', split_axis=0, concat_axis=1, tiled=True)  14.6 us
    ppermute x1, waiting for transfers between devices, from_partner(): lax.ppermute(shard, axis, [(i, i ^ 1 << stride) for i in range(lax.axis_s...  10.6 us
    dot_general x1, matrix products, body(): jnp.einsum('sgrf,sgrd->sgfd', segment.reshape(local_experts, blocks, slot...  5.85 us
    dot_general x1, matrix products, body(): jnp.einsum('srd,sfd->srf', received, w_down, preferred_element_type=jnp.f...  5.73 us
    all_to_all x1, starting transfers between devices, body(): lax.all_to_all(send_rows, 'expert', split_axis=0, concat_axis=1, tiled=True)  5.2 us
    reduce_sum x1, other arithmetic, body(): summed = jnp.sum(narrow.astype(jnp.float32), axis=1)  4.32 us
    unnamed x5, local copies, waits for them, and re-layouts  3.1 us
  transfers between devices with their start and end apart: 3, of which 2 were waited for; matrix products, arithmetic and copies ran while one was open for 6% of the time, Pallas kernels for 0%

commit v1 on v0

v1 whole, which is shorter than its diff:
```python
import functools

import jax
import jax.numpy as jnp
from jax import lax
from jax.experimental import pallas as pl
from jax.experimental.pallas import tpu as pltpu
from jax.sharding import PartitionSpec as P

MESH = pl.DeviceIdType.MESH
LANES = 128


def dot(a, b, dims):
    return lax.dot_general(a, b, (dims, ((), ())), preferred_element_type=jnp.float32)


def kernel(
    hosts, groups, capacity,
    grad_ref, ids_ref, weight_ref, flags_ref, hidden_hbm, down_hbm,
    hidden_out, down_out,
    hid, mate, wts, full, cols, table, gbuf, total, down,
    local_sem,
    zs_sem, zr_sem,
    ps_sem, pr_sem,
    ss_sem, sr_sem,
    hs_sem, hr_sem,
    ys_sem, yr_sem,
):
    half = hosts // 2
    me = lax.axis_index("expert")
    g = lax.axis_index("dp")
    core, place = lax.rem(me, 2), lax.div(me, 2)
    sibling = me + 1 - 2 * core
    partner = lax.rem(me + half, hosts)
    tokens, width = grad_ref.shape
    slots, units = hidden_hbm.shape[1:]
    share = width // groups
    count = hosts * tokens

    def to(host, group):
        return {"expert": host, "dp": group}

    def remote(src, dst, send, recv, host, group):
        return pltpu.make_async_remote_copy(
            src_ref=src, dst_ref=dst, send_sem=send, recv_sem=recv,
            device_id=(host, group), device_id_type=MESH,
        )

    def share_of(group):
        return pl.ds(pl.multiple_of(group * share, LANES), share)

    lane = lax.broadcasted_iota(jnp.int32, (tokens, LANES), 1)
    dense = jnp.zeros((tokens, LANES), jnp.float32)
    for k in range(ids_ref.shape[1]):
        dense = dense + jnp.where(ids_ref[:, k : k + 1] == lane, weight_ref[:, k : k + 1], 0.0)
    wts[g, core, place] = dense

    own = [
        pltpu.make_async_copy(grad_ref.at[:, share_of(g)], cols.at[g, core, place], local_sem.at[0]),
        pltpu.make_async_copy(grad_ref, full.at[core, place], local_sem.at[1]),
        pltpu.make_async_copy(hidden_hbm, hid.at[g], local_sem.at[2]),
        pltpu.make_async_copy(down_hbm, down, local_sem.at[3]),
    ]
    for copy in own:
        copy.start()

    barrier = pltpu.get_barrier_semaphore()

    @pl.loop(1, groups)
    def _(d):
        pl.semaphore_signal(barrier, inc=1, device_id=(me, lax.rem(g + d, groups)), device_id_type=MESH)

    @pl.loop(1, half)
    def _(d):
        pl.semaphore_signal(barrier, inc=1, device_id=(lax.rem(me + 2 * d, hosts), g), device_id_type=MESH)

    pl.semaphore_signal(barrier, inc=1, device_id=(sibling, g), device_id_type=MESH)
    pl.semaphore_wait(barrier, groups + half - 1)

    def z_copies(d, sender):
        q = lax.rem(g + groups - d, groups) if sender else lax.rem(g + d, groups)
        slot = q if sender else g
        return (
            remote(grad_ref.at[:, share_of(q)], cols.at[slot, core, place], zs_sem.at[d, 0], zr_sem.at[d, 0], me, q),
            remote(wts.at[g, core, place], wts.at[slot, core, place], zs_sem.at[d, 1], zr_sem.at[d, 1], me, q),
        )

    @pl.loop(1, groups)
    def _(d):
        for copy in z_copies(d, False):
            copy.start()

    def p_copy(d, kind, peer_place):
        peer = lax.rem(me + 2 * d, hosts)
        src, dst = (
            (grad_ref, full.at[core, peer_place]),
            (cols.at[:, core, peer_place], cols.at[:, core, peer_place]),
            (wts.at[:, core, peer_place], wts.at[:, core, peer_place]),
        )[kind]
        return remote(src, dst, ps_sem.at[d, kind], pr_sem.at[d, kind], peer, g)

    @pl.loop(1, half)
    def _(d):
        p_copy(d, 0, place).start()

    def h_copy(way, block, expert):
        target = g + 1 if way == 0 else g - 1
        part = hid.at[block, expert]
        return remote(part, part, hs_sem.at[way, block, expert], hr_sem.at[block, expert], me, target)

    def y_copy(block):
        return remote(hid.at[block, 1], mate.at[block], ys_sem.at[block], yr_sem.at[block], partner, g)

    own[2].wait()

    def forward(block, expert):
        @pl.when((g < groups - 1) & (block <= g))
        def _():
            h_copy(0, block, expert).start()

        @pl.when((g > 0) & (block >= g))
        def _():
            h_copy(1, block, expert).start()

    forward(g, 1)
    forward(g, 0)

    own[0].wait()
    own[1].wait()

    @pl.loop(1, groups)
    def _(d):
        for copy in z_copies(d, True):
            copy.wait_recv()

    @pl.loop(1, half)
    def _(d):
        p_copy(d, 1, place).start()
        p_copy(d, 2, place).start()

    y_copy(g).start()

    @pl.loop(1, half)
    def _(d):
        source = lax.rem(place + half - d, half)
        for kind in range(3):
            p_copy(d, kind, source).wait_recv()

    def s_copy(kind, c):
        src = (full.at[c], cols.at[:, c], wts.at[:, c])[kind]
        return remote(src, src, ss_sem.at[kind], sr_sem.at[kind], sibling, g)

    for kind in range(3):
        s_copy(kind, core).start()

    def arrive(block, expert):
        @pl.when((block >= 0) & (block < groups))
        def _():
            h_copy(0, block, expert).wait_recv()
            forward(block, expert)
            if expert == 1:
                y_copy(block).start()

    for block in (g - 1, g + 1):
        arrive(block, 1)

    for kind in range(3):
        s_copy(kind, 1 - core).wait_recv()

    flag = flags_ref[pl.ds(me, 1), :].astype(jnp.float32)
    shift = tokens.bit_length() - 1
    early = lax.broadcasted_iota(jnp.int32, (count, count), 0)
    late = lax.broadcasted_iota(jnp.int32, (count, count), 1)
    before = (early < late) & (lax.shift_right_logical(early, shift) == lax.shift_right_logical(late, shift))
    before = jnp.where(before, 1.0, 0.0).astype(jnp.bfloat16)
    block_of = lax.shift_right_logical(lax.broadcasted_iota(jnp.int32, (1, count), 1), shift)
    host_of = jnp.where(block_of >= half, 2 * (block_of - half) + 1, 2 * block_of)
    slot_iota = lax.broadcasted_iota(jnp.int32, (slots, count), 0)

    def selection(q, which):
        expert = 2 * (partner if which == 2 else me) + (0 if which == 0 else 1)
        weight = table[0, pl.ds(expert, 1), :]
        position = table[1, pl.ds(expert, 1), :].astype(jnp.int32)
        slot = jnp.where(weight > 0.0, host_of * capacity + position, -1)
        hit = slot_iota == slot
        pick = jnp.where(hit, 1.0, 0.0)
        held = jnp.sum(jnp.where(hit, weight, 0.0), axis=1, keepdims=True)
        return pick.astype(jnp.bfloat16), held

    def fill_table(q):
        dense = wts[q].reshape(count, LANES).T
        table[0] = dense
        chosen = jnp.where(dense > 0.0, 1.0, 0.0).astype(jnp.bfloat16)
        table[1] = dot(chosen, before, ((1,), (0,)))

    @pl.loop(0, groups)
    def _(q):
        fill_table(q)
        rows = cols[q].reshape(count, share)
        for which in range(3):
            pick, held = selection(q, which)
            scale = held if which == 0 else held * (flag if which == 2 else 1.0 - flag)
            gbuf[q, which] = (dot(pick, rows, ((1,), (0,))) * scale).astype(jnp.bfloat16)

    own[3].wait()
    fill_table(g)
    everything = full[...].reshape(count, width)
    for which in range(2):
        pick, held = selection(g, which)
        slot_rows = (dot(pick, everything, ((1,), (0,))) * held).astype(jnp.bfloat16)
        hidden_out[which] = dot(slot_rows, down[which], ((1,), (1,))).astype(hidden_out.dtype)

    for block in (g - 1, g + 1):
        arrive(block, 0)

    def first(block):
        total[0] += dot(hid[block, 0], gbuf[block, 0], ((0,), (0,)))

    def second(block):
        y_copy(block).wait_recv()
        total[1] += dot(hid[block, 1], gbuf[block, 1], ((0,), (0,)))
        total[1] += dot(mate[block], gbuf[block, 2], ((0,), (0,)))

    total[...] = jnp.zeros_like(total)
    first(g)
    second(g)

    def there(block, act):
        @pl.when((block >= 0) & (block < groups))
        def _():
            act(block)

    @pl.loop(1, groups)
    def _(k):
        @pl.when(k > 1)
        def _():
            for block in (g - k, g + k):
                arrive(block, 1)

        there(g - k + 1, lambda block: pl.when(k > 1)(functools.partial(second, block)))
        there(g + k - 1, lambda block: pl.when(k > 1)(functools.partial(second, block)))

        @pl.when(k > 1)
        def _():
            for block in (g - k, g + k):
                arrive(block, 0)

        there(g - k, first)
        there(g + k, first)

    there(g - groups + 1, second)
    there(g + groups - 1, second)
    down_out[...] = total[...].astype(down_out.dtype)

    @pl.loop(1, groups)
    def _(d):
        for copy in z_copies(d, False):
            copy.wait_send()

    @pl.loop(1, half)
    def _(d):
        for kind in range(3):
            p_copy(d, kind, place).wait_send()

    for kind in range(3):
        s_copy(kind, core).wait_send()

    @pl.loop(0, groups)
    def _(block):
        y_copy(block).wait_send()
        for expert in range(2):
            @pl.when((g < groups - 1) & (block <= g))
            def _():
                h_copy(0, block, expert).wait_send()

            @pl.when((g > 0) & (block >= g))
            def _():
                h_copy(1, block, expert).wait_send()


def body(out_grad, expert_ids, route_weights, saved_hidden, w_down, swap_flags):
    hosts, groups = lax.axis_size("expert"), lax.axis_size("dp")
    local, slots, units = saved_hidden.shape
    tokens, width = out_grad.shape
    share = width // groups
    half = hosts // 2
    vmem = pl.BlockSpec(memory_space=pltpu.VMEM)
    hbm = pl.BlockSpec(memory_space=pl.ANY)
    dma = pltpu.SemaphoreType.DMA
    return pl.pallas_call(
        functools.partial(kernel, hosts, groups, slots // hosts),
        out_shape=(
            jax.ShapeDtypeStruct((local, slots, units), jnp.bfloat16),
            jax.ShapeDtypeStruct((local, units, share), jnp.bfloat16),
        ),
        in_specs=[vmem, vmem, vmem, vmem, hbm, hbm],
        out_specs=(vmem, vmem),
        scratch_shapes=[
            pltpu.VMEM((groups, local, slots, units), jnp.bfloat16),
            pltpu.VMEM((groups, slots, units), jnp.bfloat16),
            pltpu.VMEM((groups, 2, half, tokens, LANES), jnp.float32),
            pltpu.VMEM((2, half, tokens, width), jnp.bfloat16),
            pltpu.VMEM((groups, 2, half, tokens, share), jnp.bfloat16),
            pltpu.VMEM((2, LANES, hosts * tokens), jnp.float32),
            pltpu.VMEM((groups, 3, slots, share), jnp.bfloat16),
            pltpu.VMEM((local, units, share), jnp.float32),
            pltpu.VMEM(w_down.shape, jnp.bfloat16),
            dma((4,)),
            dma((groups, 2)), dma((groups, 2)),
            dma((half, 3)), dma((half, 3)),
            dma((3,)), dma((3,)),
            dma((2, groups, 2)), dma((groups, 2)),
            dma((groups,)), dma((groups,)),
        ],
        compiler_params=pltpu.CompilerParams(
            collective_id=0, has_side_effects=True, vmem_limit_bytes=60 * 1024 * 1024
        ),
    )(out_grad, expert_ids, route_weights, swap_flags, saved_hidden, w_down)


def solution(mesh):
    in_specs = (
        P(("expert", "dp"), None),
        P(("expert", "dp"), None),
        P(("expert", "dp"), None),
        P("expert", "dp", None),
        P("expert", None, None),
        P(None, "dp"),
    )
    out_specs = (P("expert", "dp", None), P("expert", None, "dp"))
    return jax.shard_map(body, mesh=mesh, in_specs=in_specs, out_specs=out_specs, check_vma=False)
```

time: 123 us -> 49.2 us (0.40)
  the two profiles are of different devices: /device:TPU:0 before, /device:TPU:1 now
where the time goes in v1:
time: 49.2 us; the launch traced here: 48.9 us
  Pallas kernels  39.8 us (81%)
  local copies, waits for them, and re-layouts  8.44 us (17%)
  between operations  0.64 us (1%)
    pallas_call x1, Pallas kernels, body(): pl.pallas_call(functools.partial(kernel, hosts, groups, slots // hosts),...  39.8 us
    unnamed x5, local copies, waits for them, and re-layouts  8.44 us

profile of v1, /device:TPU:1, one launch (start us, length us, event | category | flops | bytes accessed | tf_op | source)
XLA Modules:
  0.0 48.9 jit_solution(12446074464790967388)
XLA Ops:
  0.6 1.3 %copy.10.flags_ref = s32[8,1]{1,0:T(8,128)} copy(s32[8,1]{0,1:T(1,128)} %param.11) | data formatting | bytes 64 | tf_op args[5]
  1.9 1.4 %copy.8.ids_ref = s32[16,8]{1,0:T(8,128)} copy(s32[16,8]{0,1:T(8,128)} %param.7) | data formatting | bytes 1024 | tf_op args[1]
  3.3 1.4 %copy.9.weight_ref = f32[16,8]{1,0:T(8,128)} copy(f32[16,8]{0,1:T(8,128)} %param.8) | data formatting | bytes 1024 | tf_op args[2]
  4.7 39.8 %shard_map.77 = (bf16[2,128,768]{2,1,0:T(8,128)(2,1)}, bf16[2,768,512]{2,1,0:T(8,128)(2,1)}) custom-call(bf16[16,2048]{1,0:T(8,128)(2,1)} %grad_ref.1, s32[16,8]{1,0:T(8,128)} %copy.8.ids_ref, f32[16,8]{1,0:T(8,128)} %copy.9.weight_ref, s32[8,1]{1,0:T(8,128)} %copy.10.flags_ref, bf16[2,128,768]{2,1,0:T(8,128)(2,1)} %hidden_hbm.1, bf16[2,768,2048]{2,1,0:T(8,128)(2,1)} %down_hbm.1), custom_call_target="tpu_custom_call" | custom-call | tf_op jit(solution)/shard_map/pallas_call | solution.py:291
  44.5 1.8 %copy.13 = bf16[2,128,768]{2,1,0:T(8,128)(2,1)} copy(bf16[2,128,768]{2,1,0:T(8,128)(2,1)} %get-tuple-element.4) | data formatting | bytes 786432
  46.3 2.7 %copy.14 = bf16[2,768,512]{2,1,0:T(8,128)(2,1)} copy(bf16[2,768,512]{2,1,0:T(8,128)(2,1)} %get-tuple-element.5) | data formatting | bytes 3145728

commit v2 on v1

--- a/solution.py
+++ b/solution.py
@@ -9,6 +9,8 @@
 
 MESH = pl.DeviceIdType.MESH
 LANES = 128
+VMEM_BYTES = 67_043_328
+SPARE = 1024 * 1024
 
 
 def dot(a, b, dims):
@@ -17,8 +19,9 @@
 
 def kernel(
     hosts, groups, capacity,
-    grad_ref, ids_ref, weight_ref, flags_ref, hidden_hbm, down_hbm,
+    grad_hbm, ids_hbm, weight_hbm, flags_hbm, hidden_hbm, down_hbm,
     hidden_out, down_out,
+    grad_ref, ids_ref, weight_ref, flags_ref,
     hid, mate, wts, full, cols, table, gbuf, total, down,
     local_sem,
     zs_sem, zr_sem,
@@ -50,19 +53,19 @@
     def share_of(group):
         return pl.ds(pl.multiple_of(group * share, LANES), share)
 
-    lane = lax.broadcasted_iota(jnp.int32, (tokens, LANES), 1)
-    dense = jnp.zeros((tokens, LANES), jnp.float32)
-    for k in range(ids_ref.shape[1]):
-        dense = dense + jnp.where(ids_ref[:, k : k + 1] == lane, weight_ref[:, k : k + 1], 0.0)
-    wts[g, core, place] = dense
-
+    small = [
+        pltpu.make_async_copy(ids_hbm, ids_ref, local_sem.at[4]),
+        pltpu.make_async_copy(weight_hbm, weight_ref, local_sem.at[5]),
+        pltpu.make_async_copy(grad_hbm, grad_ref, local_sem.at[6]),
+        pltpu.make_async_copy(flags_hbm, flags_ref, local_sem.at[7]),
+    ]
     own = [
-        pltpu.make_async_copy(grad_ref.at[:, share_of(g)], cols.at[g, core, place], local_sem.at[0]),
-        pltpu.make_async_copy(grad_ref, full.at[core, place], local_sem.at[1]),
+        pltpu.make_async_copy(grad_hbm.at[:, share_of(g)], cols.at[g, core, place], local_sem.at[0]),
+        pltpu.make_async_copy(grad_hbm, full.at[core, place], local_sem.at[1]),
         pltpu.make_async_copy(hidden_hbm, hid.at[g], local_sem.at[2]),
         pltpu.make_async_copy(down_hbm, down, local_sem.at[3]),
     ]
-    for copy in own:
+    for copy in small + own:
         copy.start()
 
     barrier = pltpu.get_barrier_semaphore()
@@ -76,6 +79,15 @@
         pl.semaphore_signal(barrier, inc=1, device_id=(lax.rem(me + 2 * d, hosts), g), device_id_type=MESH)
 
     pl.semaphore_signal(barrier, inc=1, device_id=(sibling, g), device_id_type=MESH)
+    for copy in small:
+        copy.wait()
+
+    row = lax.broadcasted_iota(jnp.int32, (LANES, tokens), 0)
+    dense = jnp.zeros((LANES, tokens), jnp.float32)
+    for k in range(ids_ref.shape[0]):
+        dense = dense + jnp.where(ids_ref[k : k + 1, :] == row, weight_ref[k : k + 1, :], 0.0)
+    wts[g, core, place] = dense.T
+
     pl.semaphore_wait(barrier, groups + half - 1)
 
     def z_copies(d, sender):
@@ -168,7 +180,8 @@
     for kind in range(3):
         s_copy(kind, 1 - core).wait_recv()
 
-    flag = flags_ref[pl.ds(me, 1), :].astype(jnp.float32)
+    lane = lax.broadcasted_iota(jnp.int32, (1, hosts), 1)
+    flag = jnp.sum(jnp.where(lane == me, flags_ref[...].astype(jnp.float32), 0.0), axis=1, keepdims=True)
     shift = tokens.bit_length() - 1
     early = lax.broadcasted_iota(jnp.int32, (count, count), 0)
     late = lax.broadcasted_iota(jnp.int32, (count, count), 1)
@@ -279,6 +292,17 @@
                 h_copy(1, block, expert).wait_send()
 
 
+def finish(hidden_in, down_in, hidden_out, down_out, sem):
+    copies = [
+        pltpu.make_async_copy(hidden_in, hidden_out, sem.at[0]),
+        pltpu.make_async_copy(down_in, down_out, sem.at[1]),
+    ]
+    for copy in copies:
+        copy.start()
+    for copy in copies:
+        copy.wait()
+
+
 def body(out_grad, expert_ids, route_weights, saved_hidden, w_down, swap_flags):
     hosts, groups = lax.axis_size("expert"), lax.axis_size("dp")
     local, slots, units = saved_hidden.shape
@@ -288,15 +312,21 @@
     vmem = pl.BlockSpec(memory_space=pltpu.VMEM)
     hbm = pl.BlockSpec(memory_space=pl.ANY)
     dma = pltpu.SemaphoreType.DMA
-    return pl.pallas_call(
+    shapes = (
+        jax.ShapeDtypeStruct((local, slots, units), jnp.bfloat16),
+        jax.ShapeDtypeStruct((local, units, share), jnp.bfloat16),
+    )
+    kept = 2 * local * units * (slots + share) + SPARE
+    results = pl.pallas_call(
         functools.partial(kernel, hosts, groups, slots // hosts),
-        out_shape=(
-            jax.ShapeDtypeStruct((local, slots, units), jnp.bfloat16),
-            jax.ShapeDtypeStruct((local, units, share), jnp.bfloat16),
-        ),
-        in_specs=[vmem, vmem, vmem, vmem, hbm, hbm],
+        out_shape=tuple(pltpu.VMEM(x.shape, x.dtype) for x in shapes),
+        in_specs=[pl.BlockSpec(memory_space=pltpu.HBM)] * 6,
         out_specs=(vmem, vmem),
         scratch_shapes=[
+            pltpu.VMEM(out_grad.shape, out_grad.dtype),
+            pltpu.VMEM(expert_ids.shape[::-1], expert_ids.dtype),
+            pltpu.VMEM(route_weights.shape[::-1], route_weights.dtype),
+            pltpu.VMEM(swap_flags.shape[::-1], swap_flags.dtype),
             pltpu.VMEM((groups, local, slots, units), jnp.bfloat16),
             pltpu.VMEM((groups, slots, units), jnp.bfloat16),
             pltpu.VMEM((groups, 2, half, tokens, LANES), jnp.float32),
@@ -306,7 +336,7 @@
             pltpu.VMEM((groups, 3, slots, share), jnp.bfloat16),
             pltpu.VMEM((local, units, share), jnp.float32),
             pltpu.VMEM(w_down.shape, jnp.bfloat16),
-            dma((4,)),
+            dma((8,)),
             dma((groups, 2)), dma((groups, 2)),
             dma((half, 3)), dma((half, 3)),
             dma((3,)), dma((3,)),
@@ -314,9 +344,17 @@
             dma((groups,)), dma((groups,)),
         ],
         compiler_params=pltpu.CompilerParams(
-            collective_id=0, has_side_effects=True, vmem_limit_bytes=60 * 1024 * 1024
+            collective_id=0, has_side_effects=True, vmem_limit_bytes=VMEM_BYTES - kept
         ),
-    )(out_grad, expert_ids, route_weights, swap_flags, saved_hidden, w_down)
+    )(out_grad, expert_ids.T, route_weights.T, swap_flags.T, saved_hidden, w_down)
+    return pl.pallas_call(
+        finish,
+        out_shape=shapes,
+        in_specs=[vmem, vmem],
+        out_specs=(hbm, hbm),
+        scratch_shapes=[dma((2,))],
+        compiler_params=pltpu.CompilerParams(vmem_limit_bytes=8 * 1024 * 1024),
+    )(*results)
 
 
 def solution(mesh):

time: 49.2 us -> 39.7 us (0.81)
  local copies, waits for them, and re-layouts: 8.44 us -> 0 us
  Pallas kernels: 39.8 us -> 38.9 us
    unnamed x5 -> x0, local copies, waits for them, and re-layouts: 8.44 us -> none
    pallas_call x1, Pallas kernels: 39.8 us -> 37.6 us  [body(): pl.pallas_call(functools.partial(kernel, hosts, groups, slots // hosts),...]
    pallas_call x0 -> x1, Pallas kernels: none -> 1.29 us  [body(): pl.pallas_call(finish, out_shape=shapes, in_specs=[vmem, vmem], out_specs...]
where the time goes in v2:
time: 39.7 us; the launch traced here: 39.5 us
  Pallas kernels  38.9 us (98%)
  between operations  0.64 us (2%)
    pallas_call x1, Pallas kernels, body(): pl.pallas_call(functools.partial(kernel, hosts, groups, slots // hosts),...  37.6 us
    pallas_call x1, Pallas kernels, body(): pl.pallas_call(finish, out_shape=shapes, in_specs=[vmem, vmem], out_specs...  1.29 us

profile of v2, /device:TPU:1, one launch (start us, length us, event | category | flops | bytes accessed | tf_op | source)
XLA Modules:
  0.0 39.5 jit_solution(6826549508210724350)
XLA Ops:
  0.6 37.6 %shard_map.77 = (bf16[2,128,768]{2,1,0:T(8,128)(2,1)S(1)}, bf16[2,768,512]{2,1,0:T(8,128)(2,1)S(1)}) custom-call(bf16[16,2048]{1,0:T(8,128)(2,1)} %grad_hbm.1, s32[8,16]{1,0:T(8,128)} %bitcast.3, f32[8,16]{1,0:T(8,128)} %bitcast.4, s32[1,8]{1,0:T(1,128)} %bitcast.5, bf16[2,128,768]{2,1,0:T(8,128)(2,1)} %hidden_hbm.1, bf16[2,768,2048]{2,1,0:T(8,128)(2,1)} %down_hbm.1), custom_call_target="tpu_custom_call" | custom-call | tf_op jit(solution)/shard_map/pallas_call | solution.py:320
  38.2 1.3 %shard_map.78 = (bf16[2,128,768]{2,1,0:T(8,128)(2,1)}, bf16[2,768,512]{2,1,0:T(8,128)(2,1)}) custom-call(bf16[2,128,768]{2,1,0:T(8,128)(2,1)S(1)} %get-tuple-element.4.hidden_in, bf16[2,768,512]{2,1,0:T(8,128)(2,1)S(1)} %get-tuple-element.5.down_in), custom_call_target="tpu_custom_call" | custom-call | tf_op jit(solution)/shard_map/pallas_call | solution.py:350

commit v3 on v2

--- a/solution.py
+++ b/solution.py
@@ -230,41 +230,51 @@
     def first(block):
         total[0] += dot(hid[block, 0], gbuf[block, 0], ((0,), (0,)))
 
+    def second_product(block):
+        y_copy(block).wait_recv()
+        return dot(hid[block, 1], gbuf[block, 1], ((0,), (0,))) + dot(mate[block], gbuf[block, 2], ((0,), (0,)))
+
     def second(block):
-        y_copy(block).wait_recv()
-        total[1] += dot(hid[block, 1], gbuf[block, 1], ((0,), (0,)))
-        total[1] += dot(mate[block], gbuf[block, 2], ((0,), (0,)))
+        total[1] += second_product(block)
 
     total[...] = jnp.zeros_like(total)
     first(g)
     second(g)
 
-    def there(block, act):
-        @pl.when((block >= 0) & (block < groups))
-        def _():
-            act(block)
-
-    @pl.loop(1, groups)
+    def around(k, act):
+        for block in (g - k, g + k):
+            @pl.when((block >= 0) & (block < groups))
+            def _():
+                act(block)
+
+    @pl.loop(2, groups)
     def _(k):
-        @pl.when(k > 1)
-        def _():
-            for block in (g - k, g + k):
-                arrive(block, 1)
-
-        there(g - k + 1, lambda block: pl.when(k > 1)(functools.partial(second, block)))
-        there(g + k - 1, lambda block: pl.when(k > 1)(functools.partial(second, block)))
-
-        @pl.when(k > 1)
-        def _():
-            for block in (g - k, g + k):
-                arrive(block, 0)
-
-        there(g - k, first)
-        there(g + k, first)
-
-    there(g - groups + 1, second)
-    there(g + groups - 1, second)
-    down_out[...] = total[...].astype(down_out.dtype)
+        for block in (g - k, g + k):
+            arrive(block, 1)
+        around(k - 1, first)
+
+        @pl.when(k == groups - 1)
+        def _():
+            around(k - 1, second)
+
+        for block in (g - k, g + k):
+            arrive(block, 0)
+
+        @pl.when(k < groups - 1)
+        def _():
+            around(k - 1, second)
+
+    edge = (g == 0) | (g == groups - 1)
+
+    @pl.when(edge)
+    def _():
+        block = jnp.where(g == 0, groups - 1, 0)
+        down_out[0] = (total[0] + dot(hid[block, 0], gbuf[block, 0], ((0,), (0,)))).astype(down_out.dtype)
+        down_out[1] = (total[1] + second_product(block)).astype(down_out.dtype)
+
+    @pl.when(jnp.logical_not(edge))
+    def _():
+        down_out[...] = total[...].astype(down_out.dtype)
 
     @pl.loop(1, groups)
     def _(d):

time: 39.7 us -> 39.6 us (level)
  no operation moved by 1% of the time
where the time goes in v3:
time: 39.6 us; the launch traced here: 39.5 us
  Pallas kernels  38.8 us (98%)
  between operations  0.64 us (2%)
    pallas_call x1, Pallas kernels, body(): pl.pallas_call(functools.partial(kernel, hosts, groups, slots // hosts),...  37.5 us
    pallas_call x1, Pallas kernels, body(): pl.pallas_call(finish, out_shape=shapes, in_specs=[vmem, vmem], out_specs...  1.29 us

profile of v3, /device:TPU:1, one launch (start us, length us, event | category | flops | bytes accessed | tf_op | source)
XLA Modules:
  0.0 39.5 jit_solution(15711047618325626522)
XLA Ops:
  0.6 37.5 %shard_map.77 = (bf16[2,128,768]{2,1,0:T(8,128)(2,1)S(1)}, bf16[2,768,512]{2,1,0:T(8,128)(2,1)S(1)}) custom-call(bf16[16,2048]{1,0:T(8,128)(2,1)} %grad_hbm.1, s32[8,16]{1,0:T(8,128)} %bitcast.3, f32[8,16]{1,0:T(8,128)} %bitcast.4, s32[1,8]{1,0:T(1,128)} %bitcast.5, bf16[2,128,768]{2,1,0:T(8,128)(2,1)} %hidden_hbm.1, bf16[2,768,2048]{2,1,0:T(8,128)(2,1)} %down_hbm.1), custom_call_target="tpu_custom_call" | custom-call | tf_op jit(solution)/shard_map/pallas_call | solution.py:330
  38.2 1.3 %shard_map.78 = (bf16[2,128,768]{2,1,0:T(8,128)(2,1)}, bf16[2,768,512]{2,1,0:T(8,128)(2,1)}) custom-call(bf16[2,128,768]{2,1,0:T(8,128)(2,1)S(1)} %get-tuple-element.4.hidden_in, bf16[2,768,512]{2,1,0:T(8,128)(2,1)S(1)} %get-tuple-element.5.down_in), custom_call_target="tpu_custom_call" | custom-call | tf_op jit(solution)/shard_map/pallas_call | solution.py:360

commit v4 on v3

--- a/solution.py
+++ b/solution.py
@@ -116,13 +116,22 @@
     def _(d):
         p_copy(d, 0, place).start()
 
+    def rows_of(part):
+        return pl.ds((part - 1) * (slots // 2), slots // 2)
+
+    def piece(block, part):
+        return hid.at[block, 0] if part == 0 else hid.at[block, 1, rows_of(part)]
+
     def h_copy(way, block, expert):
         target = g + 1 if way == 0 else g - 1
-        part = hid.at[block, expert]
+        part = piece(block, expert)
         return remote(part, part, hs_sem.at[way, block, expert], hr_sem.at[block, expert], me, target)
 
-    def y_copy(block):
-        return remote(hid.at[block, 1], mate.at[block], ys_sem.at[block], yr_sem.at[block], partner, g)
+    def y_copy(block, part):
+        return remote(
+            piece(block, part), mate.at[block, rows_of(part)],
+            ys_sem.at[block, part - 1], yr_sem.at[block, part - 1], partner, g,
+        )
 
     own[2].wait()
 
@@ -135,8 +144,8 @@
         def _():
             h_copy(1, block, expert).start()
 
-    forward(g, 1)
-    forward(g, 0)
+    for part in (1, 2, 0):
+        forward(g, part)
 
     own[0].wait()
     own[1].wait()
@@ -151,7 +160,8 @@
         p_copy(d, 1, place).start()
         p_copy(d, 2, place).start()
 
-    y_copy(g).start()
+    for part in (1, 2):
+        y_copy(g, part).start()
 
     @pl.loop(1, half)
     def _(d):
@@ -171,11 +181,12 @@
         def _():
             h_copy(0, block, expert).wait_recv()
             forward(block, expert)
-            if expert == 1:
-                y_copy(block).start()
-
-    for block in (g - 1, g + 1):
-        arrive(block, 1)
+            if expert > 0:
+                y_copy(block, expert).start()
+
+    for part in (1, 2):
+        for block in (g - 1, g + 1):
+            arrive(block, part)
 
     for kind in range(3):
         s_copy(kind, 1 - core).wait_recv()
@@ -231,7 +242,8 @@
         total[0] += dot(hid[block, 0], gbuf[block, 0], ((0,), (0,)))
 
     def second_product(block):
-        y_copy(block).wait_recv()
+        for part in (1, 2):
+            y_copy(block, part).wait_recv()
         return dot(hid[block, 1], gbuf[block, 1], ((0,), (0,))) + dot(mate[block], gbuf[block, 2], ((0,), (0,)))
 
     def second(block):
@@ -249,8 +261,9 @@
 
     @pl.loop(2, groups)
     def _(k):
-        for block in (g - k, g + k):
-            arrive(block, 1)
+        for part in (1, 2):
+            for block in (g - k, g + k):
+                arrive(block, part)
         around(k - 1, first)
 
         @pl.when(k == groups - 1)
@@ -291,8 +304,9 @@
 
     @pl.loop(0, groups)
     def _(block):
-        y_copy(block).wait_send()
-        for expert in range(2):
+        for part in (1, 2):
+            y_copy(block, part).wait_send()
+        for expert in range(3):
             @pl.when((g < groups - 1) & (block <= g))
             def _():
                 h_copy(0, block, expert).wait_send()
@@ -350,8 +364,8 @@
             dma((groups, 2)), dma((groups, 2)),
             dma((half, 3)), dma((half, 3)),
             dma((3,)), dma((3,)),
-            dma((2, groups, 2)), dma((groups, 2)),
-            dma((groups,)), dma((groups,)),
+            dma((2, groups, 3)), dma((groups, 3)),
+            dma((groups, 2)), dma((groups, 2)),
         ],
         compiler_params=pltpu.CompilerParams(
             collective_id=0, has_side_effects=True, vmem_limit_bytes=VMEM_BYTES - kept

time: 39.6 us -> 38.8 us (0.980)
  Pallas kernels: 38.8 us -> 38 us
    pallas_call x1, Pallas kernels: 37.5 us -> 36.7 us  [body(): pl.pallas_call(functools.partial(kernel, hosts, groups, slots // hosts),...]
where the time goes in v4:
time: 38.8 us; the launch traced here: 38.6 us
  Pallas kernels  38 us (98%)
  between operations  0.64 us (2%)
    pallas_call x1, Pallas kernels, body(): pl.pallas_call(functools.partial(kernel, hosts, groups, slots // hosts),...  36.7 us
    pallas_call x1, Pallas kernels, body(): pl.pallas_call(finish, out_shape=shapes, in_specs=[vmem, vmem], out_specs...  1.29 us

profile of v4, /device:TPU:1, one launch (start us, length us, event | category | flops | bytes accessed | tf_op | source)
XLA Modules:
  0.0 38.6 jit_solution(10542213909828964584)
XLA Ops:
  0.6 36.7 %shard_map.77 = (bf16[2,128,768]{2,1,0:T(8,128)(2,1)S(1)}, bf16[2,768,512]{2,1,0:T(8,128)(2,1)S(1)}) custom-call(bf16[16,2048]{1,0:T(8,128)(2,1)} %grad_hbm.1, s32[8,16]{1,0:T(8,128)} %bitcast.3, f32[8,16]{1,0:T(8,128)} %bitcast.4, s32[1,8]{1,0:T(1,128)} %bitcast.5, bf16[2,128,768]{2,1,0:T(8,128)(2,1)} %hidden_hbm.1, bf16[2,768,2048]{2,1,0:T(8,128)(2,1)} %down_hbm.1), custom_call_target="tpu_custom_call" | custom-call | tf_op jit(solution)/shard_map/pallas_call | solution.py:344
  37.3 1.3 %shard_map.78 = (bf16[2,128,768]{2,1,0:T(8,128)(2,1)}, bf16[2,768,512]{2,1,0:T(8,128)(2,1)}) custom-call(bf16[2,128,768]{2,1,0:T(8,128)(2,1)S(1)} %get-tuple-element.4.hidden_in, bf16[2,768,512]{2,1,0:T(8,128)(2,1)S(1)} %get-tuple-element.5.down_in), custom_call_target="tpu_custom_call" | custom-call | tf_op jit(solution)/shard_map/pallas_call | solution.py:374
